TPU v7x, 32 devices: a whole 2x2x4 slice. The times are simulated.
32 devices in a mesh: grp: 8 (over y, x, core), top: 4 (over z).
Axes of the slice: x: 2, y: 2, z: 4, core: 2. Of those that a mesh axis runs over, the one named last changes fastest.
Arguments:
- basis_grad: float32 [8, 4, 512, 384], P('grp', 'top'), may hold values from -6 to 6
- leaf_q: float32 [8, 4, 512, 384], P('grp', 'top'), may hold values from -0.25 to 0.25
- leaf_rinv: float32 [8, 4, 384, 384], P('grp', 'top'), may hold values from -5 to 4, as said below
- merge_q1: float32 [8, 4, 384, 384], P('grp', 'top'), may hold values from -0.3125 to 0.3125
- merge_q2: float32 [4, 384, 384], P('top', 'grp'), may hold values from -0.15625 to 0.15625
Outputs:
- data_grad: float32 [8, 4, 512, 384], P('grp', 'top')
Inputs may be any that keep to these rules, and one draw needn't show every extreme that they name: Each leaf_rinv[i,g] is upper triangular with a diagonal between 1 and 4.
All inputs are finite; a program needn't handle non-finite values.
Results may differ from a plain program's by a relative error of at most 0.00023.
Values sent between devices are 32-bit elements; how exact they have to be, the bound alone decides.
A program may use at most 64 MiB of HBM per device.

v0:
```python
import jax
import jax.numpy as jnp
from jax import lax
from jax.sharding import PartitionSpec as P


def product(former, latter, former_dim, latter_dim):
    return lax.dot_general(
        former,
        latter,
        (((former_dim,), (latter_dim,)), ((), ())),
        precision=lax.Precision.HIGH,
        preferred_element_type=jnp.float32,
    )


def symmetrize(matrix):
    return jnp.tril(matrix) + jnp.tril(matrix, -1).T


def per_device(basis_grad, leaf_q, leaf_rinv, merge_q1, merge_q2):
    cotangent = basis_grad[0, 0]
    leaf_basis = leaf_q[0, 0]
    inverse = leaf_rinv[0, 0]
    first_block = merge_q1[0, 0]
    second_factor = lax.all_gather(merge_q2[0], "grp", axis=0, tiled=True)
    projected = product(leaf_basis, cotangent, 0, 0)
    combined = product(first_block, second_factor, 1, 0)
    top_adjoint = -lax.psum(product(projected, combined, 0, 0), ("grp", "top"))
    top_sym = symmetrize(top_adjoint)
    spread = product(leaf_basis, combined, 1, 0)
    outer = product(inverse, combined, 1, 0)
    inner = cotangent + product(spread, top_sym, 1, 0)
    result = product(inner, outer, 1, 1)
    return result[None, None]


def solution(mesh):
    placed = (
        P("grp", "top", None, None),
        P("grp", "top", None, None),
        P("grp", "top", None, None),
        P("grp", "top", None, None),
        P("top", "grp", None),
    )
    return jax.shard_map(
        per_device,
        mesh=mesh,
        in_specs=placed,
        out_specs=P("grp", "top", None, None),
        check_vma=False,
    )
```

profile of v0, /device:TPU:0, one launch (start us, length us, event | category | flops | bytes accessed | tf_op | source)
XLA Modules:
  0.0 163.3 jit_solution(13517483141683757118)
XLA Ops:
  6.5 0.0 copy-start
  6.5 0.0 copy-start.2
  6.5 0.0 all-reduce.2.cloned.1.call-start
  6.5 11.9 %all-gather = f32[1,384,384]{2,1,0:T(8,128)S(1)} all-gather(f32[1,48,384]{2,1,0:T(8,128)} %param.9), channel_id=2, replica_groups=mesh['grp'=8,'top'=4] {'grp'}, dimensions={1}, use_global_device_ids=true | all-gather | bytes 663552 | tf_op jit(solution)/shard_map/all_gather | solution.py:26
  18.4 0.0 copy-done.2
  18.4 0.0 copy-start.1
  18.4 0.7 fusion.7
  19.2 0.0 copy-done
  19.2 0.4 copy-done.1
  19.6 0.8 fusion
  20.4 1.6 fusion.17
  22.0 0.0 copy-start.3
  22.0 0.0 all-reduce.2.cloned.1.call-update
  22.0 1.0 copy-done.3
  23.0 1.1 fusion.5
  24.2 1.2 fusion.2
  25.3 124.4 %all-reduce.2.cloned.1.call-done = f32[384,384]{1,0:T(8,128)} async-done(((f32[384,384]{1,0:T(8,128)}), f32[384,384]{1,0:T(8,128)}) %all-reduce.2.cloned.1.call-update) | async-done | bytes 589840 | tf_op jit(solution)/shard_map/psum | solution.py:29
  149.8 1.1 neg.3
  150.9 1.1 copy.6
  151.9 2.7 %convolution_add_fusion = f32[512,384]{1,0:T(8,128)S(1)} fusion(f32[384,512]{1,0:T(8,128)S(1)} %fusion.2, f32[1,1,512,384]{3,2,1,0:T(8,128)S(1)} %copy-done.1, f32[384,384]{0,1:T(8,128)} %copy.6, s32[384]{0:T(512)S(1)} %iota_add_fusion, f32[384,384]{1,0:T(8,128)} %all-reduce.2.cloned.1.call-done), kind=kOutput, calls=%fused_computation.1 | convolution fusion | flops 454066176 | bytes 3540480 | tf_op jit(solution)/shard_map/dot_general | solution.py:8
  154.7 1.8 %convolution_bitcast_fusion = f32[1,1,512,384]{3,2,1,0:T(8,128)} fusion(f32[512,384]{1,0:T(8,128)S(1)} %convolution_add_fusion, f32[384,384]{1,0:T(8,128)S(1)} %fusion.5), kind=kOutput, calls=%fused_computation | convolution fusion | flops 452984832 | bytes 2162688 | tf_op jit(solution)/shard_map/dot_general | solution.py:8
  (1 shorter events, 0.0 us)
Async XLA Ops:
  6.5 12.6 %copy-start = (f32[1,1,512,384]{3,2,1,0:T(8,128)S(1)}, f32[1,1,512,384]{3,2,1,0:T(8,128)}, u32[]{:S(2)}) copy-start(f32[1,1,512,384]{3,2,1,0:T(8,128)} %param.6) | copy-start | bytes 2359300
  6.5 11.9 %copy-start.2 = (f32[1,1,384,384]{3,2,1,0:T(8,128)S(1)}, f32[1,1,384,384]{3,2,1,0:T(8,128)}, u32[]{:S(2)}) copy-start(f32[1,1,384,384]{3,2,1,0:T(8,128)} %param.8) | copy-start | bytes 1769476
  6.5 143.2 %all-reduce.2.cloned.1.call-start = ((), (), s32[]{:S(2)}) async-start(), calls=%async_computation | async-start | bytes 1179648 | tf_op jit(solution)/shard_map/psum | solution.py:29
  18.4 1.1 copy-start.1
  22.0 1.1 copy-start.3
Sparse Core Ops, SparseCore 0:
  22.1 127.6 all-reduce.1
where the time goes:
time: 164 us; the launch traced here: 163 us
  waiting for transfers between devices  124 us (76%)
  between operations  13.4 us (8%)
  blocking collectives  11.9 us (7%)
  matrix products  9.86 us (6%)
  local copies, waits for them, and re-layouts  2.51 us (2%)
    psum x1, waiting for transfers between devices, per_device(): top_adjoint = -lax.psum(product(projected, combined, 0, 0), ('grp', 'top'))  124 us
    all_gather x1, blocking collectives, per_device(): second_factor = lax.all_gather(merge_q2[0], 'grp', axis=0, tiled=True)  11.9 us
    dot_general x7, matrix products, product(): lax.dot_general(former, latter, (((former_dim,), (latter_dim,)), ((), ())...  9.86 us
  transfers between devices with their start and end apart: 1, of which 1 were waited for; matrix products, arithmetic and copies ran while one was open for 1% of the time, Pallas kernels for 0%

commit v1 on v0

--- a/solution.py
+++ b/solution.py
@@ -26,7 +26,7 @@
     second_factor = lax.all_gather(merge_q2[0], "grp", axis=0, tiled=True)
     projected = product(leaf_basis, cotangent, 0, 0)
     combined = product(first_block, second_factor, 1, 0)
-    top_adjoint = -lax.psum(product(projected, combined, 0, 0), ("grp", "top"))
+    top_adjoint = -lax.psum(lax.psum(product(projected, combined, 0, 0), "top"), "grp")
     top_sym = symmetrize(top_adjoint)
     spread = product(leaf_basis, combined, 1, 0)
     outer = product(inverse, combined, 1, 0)

time: 164 us -> 133 us (0.81)
  waiting for transfers between devices: 124 us -> 94 us
    psum x1 -> x2, waiting for transfers between devices: 124 us -> 94 us  [the longest x1 56.6 us: per_device(): lax.psum(lax.psum(product(projected, combined, 0, 0), 'top'), 'grp')]
  transfers between devices with their start and end apart: 1 -> 2, of which waited for: 1 -> 2; matrix products, arithmetic and copies ran while one was open for 1% -> 2% of each run, Pallas kernels for 0% -> 0%
where the time goes in v1:
time: 133 us
  waiting for transfers between devices  94 us (71%)
  between operations  13.5 us (10%)
  blocking collectives  11.9 us (9%)
  matrix products  9.86 us (7%)
  local copies, waits for them, and re-layouts  2.46 us (2%)
    psum x1, waiting for transfers between devices, per_device(): lax.psum(lax.psum(product(projected, combined, 0, 0), 'top'), 'grp')  56.6 us
    psum x1, waiting for transfers between devices, per_device(): lax.psum(product(projected, combined, 0, 0), 'top')  37.4 us
    all_gather x1, blocking collectives, per_device(): second_factor = lax.all_gather(merge_q2[0], 'grp', axis=0, tiled=True)  11.9 us
    dot_general x7, matrix products, product(): lax.dot_general(former, latter, (((former_dim,), (latter_dim,)), ((), ())...  9.86 us
  transfers between devices with their start and end apart: 2, of which 2 were waited for; matrix products, arithmetic and copies ran while one was open for 2% of the time, Pallas kernels for 0%

profile of v1, /device:TPU:0, one launch (start us, length us, event | category | flops | bytes accessed | tf_op | source)
XLA Modules:
  0.0 132.8 jit_solution(1810101101500457952)
XLA Ops:
  6.5 0.0 copy-start
  6.5 0.0 copy-start.2
  6.5 0.0 all-reduce.3.cloned.1.call-start
  6.5 11.9 %all-gather = f32[1,384,384]{2,1,0:T(8,128)S(1)} all-gather(f32[1,48,384]{2,1,0:T(8,128)} %param.9), channel_id=2, replica_groups=mesh['grp'=8,'top'=4] {'grp'}, dimensions={1}, use_global_device_ids=true | all-gather | bytes 663552 | tf_op jit(solution)/shard_map/all_gather | solution.py:26
  18.4 0.0 copy-done.2
  18.4 0.0 copy-start.1
  18.4 0.7 fusion.7
  19.2 0.0 copy-done
  19.2 0.4 copy-done.1
  19.6 0.8 fusion
  20.4 1.6 %fusion.17 = f32[384,384]{1,0:T(8,128)} fusion(f32[384,384]{1,0:T(8,128)S(1)} %fusion, f32[384,384]{1,0:T(8,128)S(1)} %fusion.7), kind=kOutput, calls=%fused_computation.23 | convolution fusion | flops 339738624 | bytes 1769472 | tf_op jit(solution)/shard_map/dot_general | solution.py:8
  22.0 0.0 copy-start.3
  22.0 0.0 all-reduce.3.cloned.1.call-update
  22.0 0.0 all-reduce.5.cloned.1.call-start
  22.1 1.0 copy-done.3
  23.0 1.1 fusion.5
  24.2 37.4 %all-reduce.3.cloned.1.call-done = f32[384,384]{1,0:T(8,128)} async-done(((f32[384,384]{1,0:T(8,128)}), f32[384,384]{1,0:T(8,128)}) %all-reduce.3.cloned.1.call-update) | async-done | bytes 589840 | tf_op jit(solution)/shard_map/psum | solution.py:29
  61.6 0.0 all-reduce.5.cloned.1.call-update
  61.6 1.2 fusion.2
  62.8 56.6 %all-reduce.5.cloned.1.call-done = f32[384,384]{1,0:T(8,128)} async-done(((f32[384,384]{1,0:T(8,128)}), f32[384,384]{1,0:T(8,128)}) %all-reduce.5.cloned.1.call-update) | async-done | bytes 589840 | tf_op jit(solution)/shard_map/psum | solution.py:29
  119.3 1.1 neg.3
  120.4 1.1 copy.6
  121.5 2.7 %convolution_add_fusion = f32[512,384]{1,0:T(8,128)S(1)} fusion(f32[384,512]{1,0:T(8,128)S(1)} %fusion.2, f32[1,1,512,384]{3,2,1,0:T(8,128)S(1)} %copy-done.1, f32[384,384]{0,1:T(8,128)} %copy.6, s32[384]{0:T(512)S(1)} %iota_add_fusion, f32[384,384]{1,0:T(8,128)} %all-reduce.5.cloned.1.call-done), kind=kOutput, calls=%fused_computation.1 | convolution fusion | flops 454066176 | bytes 3540480 | tf_op jit(solution)/shard_map/dot_general | solution.py:8
  124.2 1.8 %convolution_bitcast_fusion = f32[1,1,512,384]{3,2,1,0:T(8,128)} fusion(f32[512,384]{1,0:T(8,128)S(1)} %convolution_add_fusion, f32[384,384]{1,0:T(8,128)S(1)} %fusion.5), kind=kOutput, calls=%fused_computation | convolution fusion | flops 452984832 | bytes 2162688 | tf_op jit(solution)/shard_map/dot_general | solution.py:8
  (1 shorter events, 0.0 us)
Async XLA Ops:
  6.5 12.6 %copy-start = (f32[1,1,512,384]{3,2,1,0:T(8,128)S(1)}, f32[1,1,512,384]{3,2,1,0:T(8,128)}, u32[]{:S(2)}) copy-start(f32[1,1,512,384]{3,2,1,0:T(8,128)} %param.6) | copy-start | bytes 2359300
  6.5 11.9 %copy-start.2 = (f32[1,1,384,384]{3,2,1,0:T(8,128)S(1)}, f32[1,1,384,384]{3,2,1,0:T(8,128)}, u32[]{:S(2)}) copy-start(f32[1,1,384,384]{3,2,1,0:T(8,128)} %param.8) | copy-start | bytes 1769476
  6.5 55.0 %all-reduce.3.cloned.1.call-start = ((), (), s32[]{:S(2)}) async-start(), calls=%async_computation | async-start | bytes 1179648 | tf_op jit(solution)/shard_map/psum | solution.py:29
  18.4 1.1 copy-start.1
  22.0 1.1 copy-start.3
  22.0 97.3 %all-reduce.5.cloned.1.call-start = ((), (), s32[]{:S(2)}) async-start(), calls=%async_computation.1 | async-start | bytes 1179648 | tf_op jit(solution)/shard_map/psum | solution.py:29
Sparse Core Ops, SparseCore 0:
  22.1 39.3 all-reduce.2
  64.7 54.5 all-reduce.4
